TPU v7x, 32 devices: a whole 2x2x4 slice. The times are simulated.
32 devices in a mesh: ia: 4 (over x, core), ja: 8 (over z, y).
Axes of the slice: x: 2, y: 2, z: 4, core: 2. Of those that a mesh axis runs over, the one named last changes fastest.
Arguments:
- star_pos: float32 [3, 32768], P(None, ('ia', 'ja')), may hold values from -6 to 6
- star_vel: float32 [3, 32768], P(None, ('ia', 'ja')), may hold values from -3 to 3
- star_acc: float32 [3, 32768], P(None, ('ia', 'ja')), may hold values from -3 to 3
- star_jerk: float32 [3, 32768], P(None, ('ia', 'ja')), may hold values from -6 to 6
- star_mass: float32 [32768], P(('ia', 'ja')), may hold values from 6.1035157e-06 to 0.00015258789
- star_level: int32 [32768], P(('ia', 'ja')), may hold values from 0 to 5, as said below
- active_index: int32 [256], P(('ia', 'ja')), may hold values from 0 to 1023, as said below
- active_count: int32 [32], P(('ia', 'ja')), may hold values from 1 to 8, as said below
Outputs:
- updated: float32 [12, 256], P(None, ('ia', 'ja'))
Inputs may be any that keep to these rules, and one draw needn't show every extreme that they name: active_count[b] is the number of active stars of owner block b; some block has exactly 8, not always the same one. `active_index`: the slots of owner block b hold distinct local star numbers of that block; the first active_count[b] of them are exactly the stars of the block with star_level 3 or more, the others name inactive stars of the block. `star_level`: A star is active at this step exactly when its level is 3 or more.
All inputs are finite; a program needn't handle non-finite values.
Results may differ from a plain program's by a relative error of at most 0.0003.
Values sent between devices are 32-bit elements; how exact they have to be, the bound alone decides.
A program may use at most 64 MiB of HBM per device.

v0:
```python
import math
import jax
import jax.numpy as jnp
from jax import lax
from jax.sharding import PartitionSpec as P

tick_now = 44
top_level = 5
tick_length = 0.125
soft_square = 0.0001


def star_age(levels):
    periods = jnp.left_shift(jnp.ones_like(levels), top_level - levels)
    remains = jnp.remainder(jnp.full_like(levels, tick_now), periods)
    ticks = jnp.where(remains == 0, periods, remains)
    return ticks.astype(jnp.float32) * tick_length


def predict(positions, velocity, accelerations, jerk_rates, star_ages):
    elapsed = star_ages[None, :]
    new_pos = positions + elapsed * (
        velocity + elapsed * (accelerations * 0.5 + elapsed * jerk_rates / 6.0)
    )
    new_vel = velocity + elapsed * (accelerations + elapsed * jerk_rates * 0.5)
    return (new_pos, new_vel)


def pair_block(targets, sources):
    delta_pos = [sources[axis_num][None, :] - targets[axis_num][:, None] for axis_num in range(3)]
    delta_vel = [
        sources[3 + axis_num][None, :] - targets[3 + axis_num][:, None] for axis_num in range(3)
    ]
    squared = (
        delta_pos[0] * delta_pos[0]
        + delta_pos[1] * delta_pos[1]
        + delta_pos[2] * delta_pos[2]
        + soft_square
    )
    inverse = lax.rsqrt(squared)
    inverse_sq = inverse * inverse
    strength = sources[6][None, :] * inverse * inverse_sq
    radial = (
        3.0
        * (delta_pos[0] * delta_vel[0] + delta_pos[1] * delta_vel[1] + delta_pos[2] * delta_vel[2])
        * inverse_sq
    )
    results = [jnp.sum(strength * delta_pos[axis_num], axis=1) for axis_num in range(3)]
    results = results + [
        jnp.sum(strength * (delta_vel[axis_num] - radial * delta_pos[axis_num]), axis=1)
        for axis_num in range(3)
    ]
    return jnp.stack(results)


def correct(targets, forces, old_acc, old_jerk, step_sizes, live_mask):
    new_acc = forces[:3]
    new_jerk = forces[3:]
    elapsed = step_sizes[None, :]
    change = old_acc - new_acc
    snap_part = -6.0 * change - elapsed * (4.0 * old_jerk + 2.0 * new_jerk)
    crackle_part = 12.0 * change + 6.0 * elapsed * (old_jerk + new_jerk)
    cor_pos = targets[:3] + elapsed * elapsed * (snap_part / 24.0 + crackle_part / 120.0)
    cor_vel = targets[3:] + elapsed * (snap_part / 6.0 + crackle_part / 24.0)
    stacked = jnp.concatenate([cor_pos, cor_vel, new_acc, new_jerk], 0)
    return jnp.where(live_mask[None, :], stacked, 0.0)


def tile_forces(targets, sources):
    slot_count = targets.shape[1]
    source_count = sources.shape[1]
    tile_rows = math.gcd(slot_count, max(32, slot_count // 16))
    tile_cols = math.gcd(source_count, max(128, 131072 // tile_rows))
    tile_count = slot_count // tile_rows
    col_turns = source_count // tile_cols
    tiles = jnp.transpose(targets.reshape(6, tile_count, tile_rows), (1, 0, 2))
    offsets = jnp.arange(tile_count, dtype=jnp.int32) * tile_rows
    zero_tile = jnp.zeros((6, tile_rows), jnp.float32)

    def compute(target_tile):

        def advance(turn_index, running):
            source_part = lax.dynamic_slice_in_dim(sources, turn_index * tile_cols, tile_cols, 1)
            return running + pair_block(target_tile, source_part)

        return lax.fori_loop(0, col_turns, advance, zero_tile)

    def one_tile(tile_entry):
        target_tile, offset = tile_entry
        return compute(target_tile)

    results = lax.map(one_tile, (tiles, offsets))
    return jnp.transpose(results, (1, 0, 2)).reshape(6, slot_count)


def arrange(targets):
    return (targets, None, None)


def on_device(
    star_pos, star_vel, star_acc, star_jerk, star_mass, star_level, active_index, active_count
):
    capacity = active_index.shape[0]
    star_ages = star_age(star_level)
    pred_pos, pred_vel = predict(star_pos, star_vel, star_acc, star_jerk, star_ages)
    sources = jnp.concatenate([pred_pos, pred_vel, star_mass[None, :]], 0)
    own_targets = jnp.concatenate(
        [jnp.take(pred_pos, active_index, axis=1), jnp.take(pred_vel, active_index, axis=1)], 0
    )
    count_value = active_count.astype(jnp.float32)
    targets, counts = (
        lax.all_gather(own_targets, "ia", axis=1, tiled=True),
        lax.all_gather(count_value, "ia", axis=0, tiled=True),
    )
    prepared, live_total, places = arrange(targets)
    pair_sums = tile_forces(prepared, lax.all_gather(sources, "ja", axis=1, tiled=True))
    forces = lax.psum_scatter(pair_sums, "ia", scatter_dimension=1, tiled=True)
    live_mask = jnp.arange(capacity, dtype=jnp.int32) < active_count[0]
    old_acc = jnp.take(star_acc, active_index, axis=1)
    old_jerk = jnp.take(star_jerk, active_index, axis=1)
    step_sizes = jnp.take(star_ages, active_index)
    return correct(own_targets, forces, old_acc, old_jerk, step_sizes, live_mask)


def solution(mesh):
    placed = (
        P(None, ("ia", "ja")),
        P(None, ("ia", "ja")),
        P(None, ("ia", "ja")),
        P(None, ("ia", "ja")),
        P(("ia", "ja")),
        P(("ia", "ja")),
        P(("ia", "ja")),
        P(("ia", "ja")),
    )
    return jax.shard_map(
        on_device, mesh=mesh, in_specs=placed, out_specs=P(None, ("ia", "ja")), check_vma=False
    )
```

profile of v0, /device:TPU:0, one launch (start us, length us, event | category | flops | bytes accessed | tf_op | source)
XLA Modules:
  0.0 60.1 jit_solution(17922956348764657168)
XLA Ops:
  0.0 0.7 %compare_select_fusion.2 = s32[8]{0:T(128)S(1)} fusion(s32[8]{0:T(128)} %param.18), kind=kLoop, calls=%fused_computation.75 | loop fusion | flops 24 | bytes 64 | tf_op jit(solution)/shard_map/jit(_take)/jit(_where)/select_n | solution.py:108
  0.7 0.1 fusion.18
  0.9 0.6 %gather_fusion = f32[8]{0:T(128)S(1)} fusion(f32[1024]{0:T(1024)S(1)} %fusion.18, s32[1024]{0:T(1024)S(1)} %pad_clamp_fusion), kind=kCustom, calls=%fused_computation.4 | custom fusion | bytes 96 | tf_op jit(solution)/shard_map/jit(_take)/gather | solution.py:121
  1.5 0.0 copy-done
  1.6 0.0 copy-done.1
  1.6 0.0 copy-done.2
  1.6 0.2 copy.76
  1.9 0.6 gather_fusion.1
  2.4 0.2 copy.78
  2.6 0.6 gather_fusion.3
  3.2 0.1 select_bitcast_fusion.1
  3.3 0.1 pad_maximum_fusion.1
  3.4 6.2 %all_gather.7 = f32[6,32]{0,1:T(8,128)S(1)} all-gather(f32[6,8]{0,1:T(8,128)S(1)} %pad_maximum_fusion.1), channel_id=1, replica_groups=mesh['ia'=4,'ja'=8] {'ia'}, dimensions={1}, use_global_device_ids=true | all-gather | bytes 960 | tf_op jit(solution)/shard_map/all_gather | solution.py:112
  9.6 0.1 copy.79
  9.7 0.6 %copy-done.4 = f32[1024]{0:T(1024)S(1)} copy-done((f32[1024]{0:T(1024)S(1)}, f32[1024]{0:T(1024)}, u32[]{:S(2)}) %copy-start.4) | copy-done | bytes 4120
  10.3 31.6 %all_gather.6 = f32[7,8192]{1,0:T(8,128)S(1)} all-gather(f32[7,1024]{1,0:T(8,128)S(1)} %pad_maximum_fusion), channel_id=1, replica_groups=mesh['ia'=4,'ja'=8] {'ja'}, dimensions={1}, use_global_device_ids=true | all-gather | bytes 258048 | tf_op jit(solution)/shard_map/all_gather | solution.py:116
  41.9 3.0 %while.21 = (s32[]{:T(128)}, f32[6,32]{1,0:T(8,128)S(1)}, f32[7,8192]{1,0:T(8,128)S(1)}, f32[6,32]{1,0:T(8,128)S(1)}, s32[]{:T(128)}, /*index=5*/s32[]{:T(128)},...) while((s32[]{:T(128)}, f32[6,32]{1,0:T(8,128)S(1)}, ...), condition=%wide.region_7.9_spmd.clone, body=%wide.region_0.8_spmd.clone.sunk | while | flops 5243085 | bytes 351265 | solution.py:86
  41.9 0.3 fusion.33
  42.2 1.1 %fusion.34 = (f32[32]{0:T(128)S(1)}, f32[32]{0:T(128)S(1)}, f32[32]{0:T(128)S(1)}, f32[32]{0:T(128)S(1)}, f32[32]{0:T(128)S(1)}, /*index=5*/f32[32]{0:T(128)S(1)}) fusion(f32[32]{0:T(128)S(1)} %get-tuple-element.220, f32[4096]{0:T(1024)S(1)} %bitcast.90, f32[32]{0:T(128)S(1)} %get-tuple-element.222, f32[4096]{0:T(1024)S(1)} %bitcast.86, ...), kind=kLoop, calls=%fused_computation.25.clone.1 | loop fusion | flops 5242688 | bytes 116224 | tf_op jit(solution)/shard_map/while/body/eval_jaxpr/while/body/eval_jaxpr/reduce_sum | solution.py:50
  43.4 0.3 fusion.33
  43.7 1.1 %fusion.34 = (f32[32]{0:T(128)S(1)}, f32[32]{0:T(128)S(1)}, f32[32]{0:T(128)S(1)}, f32[32]{0:T(128)S(1)}, f32[32]{0:T(128)S(1)}, /*index=5*/f32[32]{0:T(128)S(1)}) fusion(f32[32]{0:T(128)S(1)} %get-tuple-element.220, f32[4096]{0:T(1024)S(1)} %bitcast.90, f32[32]{0:T(128)S(1)} %get-tuple-element.222, f32[4096]{0:T(1024)S(1)} %bitcast.86, ...), kind=kLoop, calls=%fused_computation.25.clone.1 | loop fusion | flops 5242688 | bytes 116224 | tf_op jit(solution)/shard_map/while/body/eval_jaxpr/while/body/eval_jaxpr/reduce_sum | solution.py:50
  44.9 0.1 copy.80
  45.0 10.1 %all-reduce = f32[6,32]{0,1:T(8,128)S(1)} all-reduce(f32[6,32]{0,1:T(8,128)S(1)} %copy.80), channel_id=2, replica_groups=mesh['ia'=4,'ja'=8] {'ia'}, use_global_device_ids=true, to_apply=%region_8.10.clone | all-reduce | flops 192 | bytes 1536
  55.1 0.7 %copy-done.7 = u32[32]{0:T(128)S(1)} copy-done((u32[32]{0:T(128)S(1)}, u32[32]{0:T(128)}, u32[]{:S(2)}) %copy-start.7) | copy-done | bytes 152
  55.8 0.6 dynamic-slice.1
  57.0 0.2 copy.77
  57.3 0.6 gather_fusion.2
  57.8 0.2 copy.81
  58.1 0.6 gather_fusion.4
  58.6 0.1 multiply_add_fusion.3
  58.7 0.1 multiply_add_fusion.2
  59.4 0.7 %maximum_select_fusion = f32[12,8]{0,1:T(8,128)} fusion(f32[6,8]{0,1:T(8,128)S(1)} %constant_dynamic-slice_fusion.1, f32[3,8]{0,1:T(8,128)S(1)} %multiply_add_fusion.2, f32[3,8]{0,1:T(8,128)S(1)} %get-tuple-element.153, pred[8]{0:T(512)(128)(4,1)S(1)} %iota_compare_fusion), kind=kLoop, calls=%fused_computation.58 | loop fusion | flops 288 | bytes 776 | tf_op jit(solution)/shard_map/jit(_where)/select_n | solution.py:66
  (25 shorter events, 0.2 us)
Async XLA Ops:
  0.0 0.7 %copy-start.5 = (s32[1024]{0:T(1024)S(1)}, s32[1024]{0:T(1024)}, u32[]{:S(2)}) copy-start(s32[1024]{0:T(1024)} %param.17) | copy-start | bytes 12292
  0.8 0.7 %copy-start.6 = (s32[8]{0:T(128)S(1)}, s32[8]{0:T(128)}, u32[]{:S(2)}) copy-start(s32[8]{0:T(128)} %param.18) | copy-start | bytes 100
  0.8 0.7 %copy-start = (f32[3,1024]{1,0:T(4,128)S(1)}, f32[3,1024]{1,0:T(4,128)}, u32[]{:S(2)}) copy-start(f32[3,1024]{1,0:T(4,128)} %param.14) | copy-start | bytes 36868
  0.8 0.7 %copy-start.1 = (f32[3,1024]{1,0:T(4,128)S(1)}, f32[3,1024]{1,0:T(4,128)}, u32[]{:S(2)}) copy-start(f32[3,1024]{1,0:T(4,128)} %param.15) | copy-start | bytes 36868
  0.9 0.7 %copy-start.2 = (f32[3,1024]{1,0:T(4,128)S(1)}, f32[3,1024]{1,0:T(4,128)}, u32[]{:S(2)}) copy-start(f32[3,1024]{1,0:T(4,128)} %param.12) | copy-start | bytes 36868
  0.9 0.7 %copy-start.3 = (f32[3,1024]{1,0:T(4,128)S(1)}, f32[3,1024]{1,0:T(4,128)}, u32[]{:S(2)}) copy-start(f32[3,1024]{1,0:T(4,128)} %param.13) | copy-start | bytes 36868
  9.6 0.7 %copy-start.4 = (f32[1024]{0:T(1024)S(1)}, f32[1024]{0:T(1024)}, u32[]{:S(2)}) copy-start(f32[1024]{0:T(1024)} %param.16) | copy-start | bytes 12292
  55.1 0.7 %copy-start.7 = (u32[32]{0:T(128)S(1)}, u32[32]{0:T(128)}, u32[]{:S(2)}) copy-start(u32[32]{0:T(128)} %constant.128) | copy-start | bytes 388
where the time goes:
time: 60.5 us; the launch traced here: 60.1 us
  blocking collectives  48 us (79%)
  local copies, waits for them, and re-layouts  6.49 us (11%)
  other arithmetic  4.14 us (7%)
  between operations  1.45 us (2%)
    all_gather x1, blocking collectives, on_device(): lax.all_gather(sources, 'ja', axis=1, tiled=True)  31.6 us
    unnamed x1, blocking collectives  10.1 us
    all_gather x1, blocking collectives, on_device(): lax.all_gather(own_targets, 'ia', axis=1, tiled=True)  6.23 us
    unnamed x21, local copies, waits for them, and re-layouts  2.47 us
    reduce_sum x2, other arithmetic, pair_block(): jnp.sum(strength * (delta_vel[axis_num] - radial * delta_pos[axis_num]),...  2.3 us

commit v1 on v0

--- a/solution.py
+++ b/solution.py
@@ -8,6 +8,18 @@
 top_level = 5
 tick_length = 0.125
 soft_square = 0.0001
+
+
+def gather_by_bits(x, axis, dim):
+    ways, here = (lax.axis_size(axis), lax.axis_index(axis))
+    grown, reach = (x, 1)
+    while reach < ways:
+        theirs = lax.ppermute(grown, axis, [(d, d ^ reach) for d in range(ways)])
+        mine_first = jnp.concatenate([grown, theirs], axis=dim)
+        theirs_first = jnp.concatenate([theirs, grown], axis=dim)
+        grown = jnp.where(here & reach == 0, mine_first, theirs_first)
+        reach = 2 * reach
+    return grown
 
 
 def star_age(levels):
@@ -109,7 +121,7 @@
     )
     count_value = active_count.astype(jnp.float32)
     targets, counts = (
-        lax.all_gather(own_targets, "ia", axis=1, tiled=True),
+        gather_by_bits(own_targets, "ia", 1),
         lax.all_gather(count_value, "ia", axis=0, tiled=True),
     )
     prepared, live_total, places = arrange(targets)

time: 60.5 us -> 57.3 us (0.947)
  blocking collectives: 48 us -> 42.3 us
  starting transfers between devices: 0 us -> 2 us
  waiting for transfers between devices: 0 us -> 0.72 us
    all_gather x1 -> x0, blocking collectives: 6.23 us -> none  [on_device(): lax.all_gather(own_targets, 'ia', axis=1, tiled=True)]
    ppermute x0 -> x2, starting transfers between devices: none -> 2 us  [gather_by_bits(): theirs = lax.ppermute(grown, axis, [(d, d ^ reach) for d in range(ways)])]
    ppermute x0 -> x2, waiting for transfers between devices: none -> 0.72 us  [gather_by_bits(): theirs = lax.ppermute(grown, axis, [(d, d ^ reach) for d in range(ways)])]
    unnamed x21 -> x20, local copies, waits for them, and re-layouts: 2.47 us -> 1.89 us
  transfers between devices with their start and end apart: 0 -> 2, of which waited for: 0 -> 1; matrix products, arithmetic and copies ran while one was open for 0% -> 4% of each run, Pallas kernels for 0% -> 0%
where the time goes in v1:
time: 57.3 us; the launch traced here: 56.9 us
  blocking collectives  42.3 us (74%)
  local copies, waits for them, and re-layouts  6.06 us (11%)
  other arithmetic  4.31 us (8%)
  starting transfers between devices  2 us (3%)
  between operations  1.5 us (3%)
  waiting for transfers between devices  0.72 us (1%)
    all_gather x1, blocking collectives, on_device(): lax.all_gather(sources, 'ja', axis=1, tiled=True)  32.2 us
    unnamed x1, blocking collectives  10.1 us
    reduce_sum x2, other arithmetic, pair_block(): jnp.sum(strength * (delta_vel[axis_num] - radial * delta_pos[axis_num]),...  2.3 us
    ppermute x2, starting transfers between devices, gather_by_bits(): theirs = lax.ppermute(grown, axis, [(d, d ^ reach) for d in range(ways)])  2 us
    unnamed x20, local copies, waits for them, and re-layouts  1.89 us
  transfers between devices with their start and end apart: 2, of which 1 were waited for; matrix products, arithmetic and copies ran while one was open for 4% of the time, Pallas kernels for 0%

profile of v1, /device:TPU:0, one launch (start us, length us, event | category | flops | bytes accessed | tf_op | source)
XLA Modules:
  0.0 56.9 jit_solution(12635065567360904768)
XLA Ops:
  0.0 0.7 %compare_select_fusion.2 = s32[8]{0:T(128)S(1)} fusion(s32[8]{0:T(128)} %param.18), kind=kLoop, calls=%fused_computation.77 | loop fusion | flops 24 | bytes 64 | tf_op jit(solution)/shard_map/jit(_take)/jit(_where)/select_n | solution.py:120
  0.7 0.1 fusion.18
  0.9 0.6 %gather_fusion = f32[8]{0:T(128)S(1)} fusion(f32[1024]{0:T(1024)S(1)} %fusion.18, s32[1024]{0:T(1024)S(1)} %pad_clamp_fusion), kind=kCustom, calls=%fused_computation.4 | custom fusion | bytes 96 | tf_op jit(solution)/shard_map/jit(_take)/gather | solution.py:133
  1.6 0.2 copy.82
  1.9 0.6 gather_fusion.1
  2.4 0.2 copy.84
  2.6 0.6 gather_fusion.3
  3.2 0.1 select_bitcast_fusion.1
  3.3 0.1 pad_maximum_fusion.1
  3.4 0.5 collective-permute-start
  3.9 0.2 copy.83
  4.1 0.2 copy.90
  4.3 0.7 %copy-done.4 = f32[1024]{0:T(1024)S(1)} copy-done((f32[1024]{0:T(1024)S(1)}, f32[1024]{0:T(1024)}, u32[]{:S(2)}) %copy-start.4) | copy-done | bytes 4120
  5.0 32.2 %all_gather.3 = f32[7,8192]{1,0:T(8,128)S(1)} all-gather(f32[7,1024]{1,0:T(8,128)S(1)} %pad_maximum_fusion), channel_id=1, replica_groups=mesh['ia'=4,'ja'=8] {'ja'}, dimensions={1}, use_global_device_ids=true | all-gather | bytes 258048 | tf_op jit(solution)/shard_map/all_gather | solution.py:128
  37.2 0.6 gather_fusion.2
  38.4 0.6 gather_fusion.4
  39.0 0.1 maximum_select_fusion
  39.1 1.5 %collective-permute-start.1 = (f32[6,16]{0,1:T(8,128)S(1)}, f32[6,16]{0,1:T(8,128)S(1)}, u32[]{:S(2)}, u32[]{:S(2)}) collective-permute-start(f32[6,16]{0,1:T(8,128)S(1)} %maximum_select_fusion), channel_id=1, source_target_pairs={{0,16},{8,24},{16,0},{24,8},{1,17},{9,25},{17,1},{25,9},{2,18},{10... | collective-permute-start | bytes 1160 | tf_op jit(solution)/shard_map/ppermute | solution.py:17
  40.6 0.7 %dynamic-slice.1 = u32[1]{0:T(128)} dynamic-slice(u32[32]{0:T(128)S(1)} %copy-done.7, u32[]{:T(128)S(6)} %add.147), dynamic_slice_sizes={1} | dynamic-slice | bytes 12
  41.9 0.1 copy.85
  42.0 0.7 %collective-permute-done.1 = f32[6,16]{0,1:T(8,128)S(1)} collective-permute-done((f32[6,16]{0,1:T(8,128)S(1)}, f32[6,16]{0,1:T(8,128)S(1)}, u32[]{:S(2)}, u32[]{:S(2)}) %collective-permute-start.1) | collective-permute-done | bytes 416 | tf_op jit(solution)/shard_map/ppermute | solution.py:17
  42.7 0.1 copy.86
  42.8 0.1 maximum_select_fusion.1
  42.9 3.0 %while.21 = (s32[]{:T(128)}, f32[6,32]{1,0:T(8,128)S(1)}, f32[7,8192]{1,0:T(8,128)S(1)}, f32[6,32]{1,0:T(8,128)S(1)}, s32[]{:T(128)}, /*index=5*/s32[]{:T(128)},...) while((s32[]{:T(128)}, f32[6,32]{1,0:T(8,128)S(1)}, ...), condition=%wide.region_7.9_spmd.clone, body=%wide.region_0.8_spmd.clone.sunk | while | flops 5243085 | bytes 351265 | solution.py:98
  42.9 0.3 fusion.33
  43.2 1.1 %fusion.34 = (f32[32]{0:T(128)S(1)}, f32[32]{0:T(128)S(1)}, f32[32]{0:T(128)S(1)}, f32[32]{0:T(128)S(1)}, f32[32]{0:T(128)S(1)}, /*index=5*/f32[32]{0:T(128)S(1)}) fusion(f32[32]{0:T(128)S(1)} %get-tuple-element.208, f32[4096]{0:T(1024)S(1)} %bitcast.90, f32[32]{0:T(128)S(1)} %get-tuple-element.210, f32[4096]{0:T(1024)S(1)} %bitcast.86, ...), kind=kLoop, calls=%fused_computation.25.clone.1 | loop fusion | flops 5242688 | bytes 116224 | tf_op jit(solution)/shard_map/while/body/eval_jaxpr/while/body/eval_jaxpr/reduce_sum | solution.py:62
  44.4 0.3 fusion.33
  44.7 1.1 %fusion.34 = (f32[32]{0:T(128)S(1)}, f32[32]{0:T(128)S(1)}, f32[32]{0:T(128)S(1)}, f32[32]{0:T(128)S(1)}, f32[32]{0:T(128)S(1)}, /*index=5*/f32[32]{0:T(128)S(1)}) fusion(f32[32]{0:T(128)S(1)} %get-tuple-element.208, f32[4096]{0:T(1024)S(1)} %bitcast.90, f32[32]{0:T(128)S(1)} %get-tuple-element.210, f32[4096]{0:T(1024)S(1)} %bitcast.86, ...), kind=kLoop, calls=%fused_computation.25.clone.1 | loop fusion | flops 5242688 | bytes 116224 | tf_op jit(solution)/shard_map/while/body/eval_jaxpr/while/body/eval_jaxpr/reduce_sum | solution.py:62
  45.9 0.1 copy.89
  46.0 10.1 %all-reduce = f32[6,32]{0,1:T(8,128)S(1)} all-reduce(f32[6,32]{0,1:T(8,128)S(1)} %copy.89), channel_id=2, replica_groups=mesh['ia'=4,'ja'=8] {'ia'}, use_global_device_ids=true, to_apply=%region_8.10.clone | all-reduce | flops 192 | bytes 1536
  56.1 0.1 multiply_add_fusion.3
  56.2 0.7 %maximum_select_fusion.2 = f32[12,8]{0,1:T(8,128)} fusion(f32[6,8]{0,1:T(8,128)S(1)} %constant_dynamic-slice_fusion.1, f32[3,8]{0,1:T(8,128)S(1)} %multiply_add_fusion.2, f32[3,8]{0,1:T(8,128)S(1)} %get-tuple-element.141, pred[8]{0:T(512)(128)(4,1)S(1)} %iota_compare_fusion), kind=kLoop, calls=%fused_computation.60 | loop fusion | flops 288 | bytes 776 | tf_op jit(solution)/shard_map/jit(_where)/select_n | solution.py:78
  (31 shorter events, 0.3 us)
Async XLA Ops:
  0.0 0.7 %copy-start.5 = (s32[1024]{0:T(1024)S(1)}, s32[1024]{0:T(1024)}, u32[]{:S(2)}) copy-start(s32[1024]{0:T(1024)} %param.17) | copy-start | bytes 12292
  0.8 0.7 %copy-start.6 = (s32[8]{0:T(128)S(1)}, s32[8]{0:T(128)}, u32[]{:S(2)}) copy-start(s32[8]{0:T(128)} %param.18) | copy-start | bytes 100
  0.8 0.7 %copy-start = (f32[3,1024]{1,0:T(4,128)S(1)}, f32[3,1024]{1,0:T(4,128)}, u32[]{:S(2)}) copy-start(f32[3,1024]{1,0:T(4,128)} %param.14) | copy-start | bytes 36868
  0.8 0.7 %copy-start.1 = (f32[3,1024]{1,0:T(4,128)S(1)}, f32[3,1024]{1,0:T(4,128)}, u32[]{:S(2)}) copy-start(f32[3,1024]{1,0:T(4,128)} %param.15) | copy-start | bytes 36868
  0.9 0.7 %copy-start.2 = (f32[3,1024]{1,0:T(4,128)S(1)}, f32[3,1024]{1,0:T(4,128)}, u32[]{:S(2)}) copy-start(f32[3,1024]{1,0:T(4,128)} %param.12) | copy-start | bytes 36868
  0.9 0.7 %copy-start.3 = (f32[3,1024]{1,0:T(4,128)S(1)}, f32[3,1024]{1,0:T(4,128)}, u32[]{:S(2)}) copy-start(f32[3,1024]{1,0:T(4,128)} %param.13) | copy-start | bytes 36868
  3.4 35.6 %collective-permute-start = (f32[6,8]{0,1:T(8,128)S(1)}, f32[6,8]{0,1:T(8,128)S(1)}, u32[]{:S(2)}, u32[]{:S(2)}) collective-permute-start(f32[6,8]{0,1:T(8,128)S(1)} %pad_maximum_fusion.1), channel_id=1, source_target_pairs={{0,8},{8,0},{16,24},{24,16},{1,9},{9,1},{17,25},{25,17},{2,10},{10... | collective-permute-start | bytes 584 | tf_op jit(solution)/shard_map/ppermute | solution.py:17
  4.3 0.7 %copy-start.4 = (f32[1024]{0:T(1024)S(1)}, f32[1024]{0:T(1024)}, u32[]{:S(2)}) copy-start(f32[1024]{0:T(1024)} %param.16) | copy-start | bytes 12292
  39.1 1.5 %copy-start.7 = (u32[32]{0:T(128)S(1)}, u32[32]{0:T(128)}, u32[]{:S(2)}) copy-start(u32[32]{0:T(128)} %constant.136) | copy-start | bytes 388
  39.1 3.7 %collective-permute-start.1 = (f32[6,16]{0,1:T(8,128)S(1)}, f32[6,16]{0,1:T(8,128)S(1)}, u32[]{:S(2)}, u32[]{:S(2)}) collective-permute-start(f32[6,16]{0,1:T(8,128)S(1)} %maximum_select_fusion), channel_id=1, source_target_pairs={{0,16},{8,24},{16,0},{24,8},{1,17},{9,25},{17,1},{25,9},{2,18},{10... | collective-permute-start | bytes 1160 | tf_op jit(solution)/shard_map/ppermute | solution.py:17
